TPU v7x, 256 devices: a whole 4x4x8 slice. The times are simulated.
256 devices in a mesh: row: 16 (over x_lo, y, core), col: 16 (over x_hi, z).
Axes of the slice: x: 4 (x_hi: 2, x_lo: 2; x = x_hi * 2 + x_lo), y: 4, z: 8, core: 2. Of those that a mesh axis runs over, the one named last changes fastest.
Arguments:
- node_features: bfloat16 [65536, 256], P(('row', 'col')), may hold values from -6 to 6
- tile_values: bfloat16 [16, 16, 128, 128, 128], P('row', 'col'), may hold values from -0.09375 to 0.09375
- tile_coords: int32 [16, 16, 128, 2], P('row', 'col'), may hold values from 0 to 31, as said below
- tile_counts: int32 [16, 16], P('row', 'col'), may hold values from 32 to 128, as said below
- first_weight: bfloat16 [256, 256], replicated, may hold values from -0.375 to 0.375
- second_weight: bfloat16 [256, 128], replicated, may hold values from -0.375 to 0.375
- out_grad: bfloat16 [65536, 128], P(('row', 'col')), may hold values from -6 to 6
Outputs:
- output: bfloat16 [65536, 128], P(('row', 'col'))
- first_grad: float32 [256, 256], replicated
- second_grad: float32 [256, 128], replicated
Inputs may be any that keep to these rules, and one draw needn't show every extreme that they name: `tile_counts`: each grid cell uses at least 32 slots; at least one grid cell uses all 128 in every draw. `tile_coords`: the first entry is a tile row below 32, the second a tile column below 32; within one grid cell no two slots share a position.
All inputs are finite; a program needn't handle non-finite values.
Results may differ from a plain program's by a relative error of at most 0.005.
Values may be sent and summed in bfloat16 or wider, within the bound.
A program may use at most 64 MiB of HBM per device.

v0:
```python
import math
import jax
import jax.numpy as jnp
from jax import lax
from jax.sharding import PartitionSpec as P

HIGHEST = lax.Precision.HIGHEST


def tile_sum(tile_block, dest_index, source_index, live_slots, source, dest_tiles, flipped):
    slot_count = tile_block.shape[0]
    group_size = math.gcd(slot_count, 32)
    round_count = slot_count // group_size
    edge_size = tile_block.shape[1]
    width_size = source.shape[-1]
    grouped_tiles = tile_block.reshape(round_count, group_size, edge_size, edge_size)
    grouped_dest = dest_index.reshape(round_count, group_size)
    grouped_source = source_index.reshape(round_count, group_size)
    grouped_live = live_slots.reshape(round_count, group_size)
    target_ids = jnp.arange(dest_tiles, dtype=jnp.int32)
    einsum_form = "tba,tbw->taw" if flipped else "tab,tbw->taw"

    def add_group(running, pieces):
        group_tiles, group_dest, group_source, group_live = pieces
        picked = jnp.take(source, group_source, axis=0)
        products = jnp.einsum(einsum_form, group_tiles, picked, preferred_element_type=jnp.float32)
        select = ((group_dest[:, None] == target_ids[None, :]) & group_live[:, None]).astype(
            jnp.float32
        )
        running = running + jnp.einsum("tr,taw->raw", select, products, precision=HIGHEST)
        return (running, None)

    start_sum = jnp.zeros((dest_tiles, edge_size, width_size), jnp.float32)
    running, unused = lax.scan(
        add_group, start_sum, (grouped_tiles, grouped_dest, grouped_source, grouped_live)
    )
    return running.reshape(dest_tiles * edge_size, width_size)


def on_device(
    node_features, tile_values, tile_coords, tile_counts, first_weight, second_weight, out_grad
):
    node_rows = node_features.shape[0]
    edge_size = tile_values.shape[-1]
    slot_count = tile_values.shape[2]
    grid_rows = lax.axis_size("row")
    grid_cols = lax.axis_size("col")
    row_tiles = grid_rows * node_rows // edge_size
    col_tiles = grid_cols * node_rows // edge_size
    tile_block = tile_values.reshape(slot_count, edge_size, edge_size)
    flat_coords = tile_coords.reshape(slot_count, 2)
    tile_row = flat_coords[:, 0]
    tile_col = flat_coords[:, 1]
    live_slots = jnp.arange(slot_count, dtype=jnp.int32) < tile_counts.reshape(())
    gathered_x = lax.all_gather(node_features, "col", axis=0, tiled=True)
    feature_part = tile_sum(
        tile_block,
        tile_row,
        tile_col,
        live_slots,
        gathered_x.reshape(col_tiles, edge_size, -1),
        row_tiles,
        False,
    )
    first_mean = lax.psum_scatter(feature_part, "row", scatter_dimension=0, tiled=True)
    first_pre = jnp.dot(first_mean, first_weight.astype(jnp.float32), precision=HIGHEST)
    hidden_act = jax.nn.silu(first_pre).astype(jnp.bfloat16)
    second_wide = second_weight.astype(jnp.float32)
    gathered_h = lax.all_gather(hidden_act, "col", axis=0, tiled=True)
    hidden_part = tile_sum(
        tile_block,
        tile_row,
        tile_col,
        live_slots,
        gathered_h.reshape(col_tiles, edge_size, -1),
        row_tiles,
        False,
    )
    second_mean = lax.psum_scatter(hidden_part, "row", scatter_dimension=0, tiled=True)
    logit_rows = jnp.dot(second_mean, second_wide, precision=HIGHEST)
    output = logit_rows.astype(jnp.bfloat16)
    gathered_g = lax.all_gather(out_grad, "row", axis=0, tiled=True)
    grad_part = tile_sum(
        tile_block,
        tile_col,
        tile_row,
        live_slots,
        gathered_g.reshape(row_tiles, edge_size, -1),
        col_tiles,
        True,
    )
    back_sum = lax.psum_scatter(grad_part, "col", scatter_dimension=0, tiled=True)
    scale = 1.0 / math.sqrt(node_rows * grid_rows * grid_cols)
    second_local = jnp.dot(hidden_act.astype(jnp.float32).T, back_sum, precision=HIGHEST) * scale
    hidden_grad = jnp.dot(back_sum, second_wide.T, precision=HIGHEST)
    sigma = jax.nn.sigmoid(first_pre)
    pre_grad = hidden_grad * (sigma * (1.0 + first_pre * (1.0 - sigma)))
    second_grad = lax.psum(second_local, ("row", "col"))
    first_local = jnp.dot(first_mean.T, pre_grad, precision=HIGHEST) * scale
    first_grad = lax.psum(first_local, ("row", "col"))
    return (output, first_grad, second_grad)


def solution(mesh):
    return jax.shard_map(
        on_device,
        mesh=mesh,
        in_specs=(
            P(("row", "col"), None),
            P("row", "col", None, None, None),
            P("row", "col", None, None),
            P("row", "col"),
            P(),
            P(),
            P(("row", "col"), None),
        ),
        out_specs=(P(("row", "col"), None), P(), P()),
        check_vma=False,
    )
```

profile of v0, /device:TPU:1, one launch (start us, length us, event | category | flops | bytes accessed | tf_op | source)
XLA Modules:
  0.0 898.8 jit_solution(9143985936863349914)
XLA Ops:
  9.6 86.8 %all-gather.4.cloned.1.call-done = bf16[4096,256]{1,0:T(8,128)(2,1)} async-done(((bf16[256,256]{1,0:T(8,128)(2,1)}), bf16[4096,256]{1,0:T(8,128)(2,1)}) %all-gather.4.cloned.1.call-update) | async-done | bytes 2097168 | tf_op jit(solution)/shard_map/all_gather | solution.py:55
  96.3 64.7 %while.33 = (s32[]{:T(128)}, f32[32,128,256]{2,0,1:T(8,128)}, s32[4,32]{1,0:T(4,128)S(1)}, pred[4,32]{1,0:T(4,128)(4,1)S(1)}, bf16[4,32,128,128]{3,2,1,0:T(8,128...) while((s32[]{:T(128)}, f32[32,128,256]{2,0,1:T(8,128)}, ...), condition=%wide.region_1.3_spmd.clone, body=%wide.region_0.2_spmd.clone.sunk | while | flops 674237632 | bytes 24123028 | solution.py:34
  102.6 8.9 select_add_fusion.6
  117.9 10.2 %select_add_fusion.6 = f32[32,128,256]{2,0,1:T(8,128)} fusion(f32[32,128,256]{2,0,1:T(8,128)} %get-tuple-element.410, f32[32,128,256]{2,1,0:T(8,128)} %fusion.96, pred[]{:T(512)S(6)} %compare.9, s32[32]{0:T(128)S(1)} %fusion.97, pred[32]{0:T(512)(128)(4,1)S(1)} %dynamic-slice_bitcast_fusion.6), kind=kOutput, calls=%fused_computation.33.clone.1 | convolution fusion | flops 404752384 | bytes 12583073 | tf_op jit(solution)/shard_map/while/body/eval_jaxpr/tr,taw->raw/dot_general | solution.py:30
  134.4 10.2 %select_add_fusion.6 = f32[32,128,256]{2,0,1:T(8,128)} fusion(f32[32,128,256]{2,0,1:T(8,128)} %get-tuple-element.410, f32[32,128,256]{2,1,0:T(8,128)} %fusion.96, pred[]{:T(512)S(6)} %compare.9, s32[32]{0:T(128)S(1)} %fusion.97, pred[32]{0:T(512)(128)(4,1)S(1)} %dynamic-slice_bitcast_fusion.6), kind=kOutput, calls=%fused_computation.33.clone.1 | convolution fusion | flops 404752384 | bytes 12583073 | tf_op jit(solution)/shard_map/while/body/eval_jaxpr/tr,taw->raw/dot_general | solution.py:30
  150.9 10.2 %select_add_fusion.6 = f32[32,128,256]{2,0,1:T(8,128)} fusion(f32[32,128,256]{2,0,1:T(8,128)} %get-tuple-element.410, f32[32,128,256]{2,1,0:T(8,128)} %fusion.96, pred[]{:T(512)S(6)} %compare.9, s32[32]{0:T(128)S(1)} %fusion.97, pred[32]{0:T(512)(128)(4,1)S(1)} %dynamic-slice_bitcast_fusion.6), kind=kOutput, calls=%fused_computation.33.clone.1 | convolution fusion | flops 404752384 | bytes 12583073 | tf_op jit(solution)/shard_map/while/body/eval_jaxpr/tr,taw->raw/dot_general | solution.py:30
  161.0 6.6 copy.10
  168.5 65.5 %reduce-scatter.4.cloned.1.call-done = f32[256,256]{1,0:T(8,128)} async-done(((f32[4096,256]{1,0:T(8,128)}), f32[256,256]{1,0:T(8,128)}) %reduce-scatter.4.cloned.1.call-update) | async-done | bytes 262160 | tf_op jit(solution)/shard_map/reduce_scatter | solution.py:65
  236.2 37.0 %all-gather.8.cloned.1.call-done = bf16[4096,128]{1,0:T(8,128)(2,1)} async-done(((bf16[256,128]{1,0:T(8,128)(2,1)}), bf16[4096,128]{1,0:T(8,128)(2,1)}) %all-gather.8.cloned.1.call-update) | async-done | bytes 1048592 | tf_op jit(solution)/shard_map/all_gather | solution.py:82
  273.2 35.7 %while.35 = (s32[]{:T(128)}, f32[32,128,128]{2,0,1:T(8,128)}, s32[4,32]{1,0:T(4,128)S(1)}, pred[4,32]{1,0:T(4,128)(4,1)S(1)}, bf16[4,32,128,128]{3,2,1,0:T(8,128...) while((s32[]{:T(128)}, f32[32,128,128]{2,0,1:T(8,128)}, ...), condition=%wide.region_7.9_spmd.clone, body=%wide.region_6.8_spmd.clone.sunk | while | flops 337120544 | bytes 12588823 | solution.py:34
  284.7 5.4 select_add_fusion.8
  294.0 5.5 select_add_fusion.8
  303.4 5.5 select_add_fusion.8
  308.8 4.2 copy.12
  313.0 44.8 %all-gather.6.cloned.1.call-done = bf16[4096,256]{1,0:T(8,128)(2,1)} async-done(((bf16[256,256]{1,0:T(8,128)(2,1)}), bf16[4096,256]{1,0:T(8,128)(2,1)}) %all-gather.6.cloned.1.call-update) | async-done | bytes 2097168 | tf_op jit(solution)/shard_map/all_gather | solution.py:69
  357.8 65.0 %while.34 = (s32[]{:T(128)}, f32[32,128,256]{2,0,1:T(8,128)}, s32[4,32]{1,0:T(4,128)S(1)}, pred[4,32]{1,0:T(4,128)(4,1)S(1)}, bf16[4,32,128,128]{3,2,1,0:T(8,128...) while((s32[]{:T(128)}, f32[32,128,256]{2,0,1:T(8,128)}, ...), condition=%wide.region_4.6_spmd.clone, body=%wide.region_3.5_spmd.clone.sunk | while | flops 674237632 | bytes 24123028 | solution.py:34
  364.1 8.9 select_add_fusion.7
  379.4 10.2 %select_add_fusion.7 = f32[32,128,256]{2,0,1:T(8,128)} fusion(f32[32,128,256]{2,0,1:T(8,128)} %get-tuple-element.437, f32[32,128,256]{2,1,0:T(8,128)} %fusion.102, pred[]{:T(512)S(6)} %compare.10, s32[32]{0:T(128)S(1)} %fusion.103, pred[32]{0:T(512)(128)(4,1)S(1)} %dynamic-slice_bitcast_fusion.7), kind=kOutput, calls=%fused_computation.57.clone.1 | convolution fusion | flops 404752384 | bytes 12583073 | tf_op jit(solution)/shard_map/while/body/eval_jaxpr/tr,taw->raw/dot_general | solution.py:30
  396.0 10.3 %select_add_fusion.7 = f32[32,128,256]{2,0,1:T(8,128)} fusion(f32[32,128,256]{2,0,1:T(8,128)} %get-tuple-element.437, f32[32,128,256]{2,1,0:T(8,128)} %fusion.102, pred[]{:T(512)S(6)} %compare.10, s32[32]{0:T(128)S(1)} %fusion.103, pred[32]{0:T(512)(128)(4,1)S(1)} %dynamic-slice_bitcast_fusion.7), kind=kOutput, calls=%fused_computation.57.clone.1 | convolution fusion | flops 404752384 | bytes 12583073 | tf_op jit(solution)/shard_map/while/body/eval_jaxpr/tr,taw->raw/dot_general | solution.py:30
  412.6 10.2 %select_add_fusion.7 = f32[32,128,256]{2,0,1:T(8,128)} fusion(f32[32,128,256]{2,0,1:T(8,128)} %get-tuple-element.437, f32[32,128,256]{2,1,0:T(8,128)} %fusion.102, pred[]{:T(512)S(6)} %compare.10, s32[32]{0:T(128)S(1)} %fusion.103, pred[32]{0:T(512)(128)(4,1)S(1)} %dynamic-slice_bitcast_fusion.7), kind=kOutput, calls=%fused_computation.57.clone.1 | convolution fusion | flops 404752384 | bytes 12583073 | tf_op jit(solution)/shard_map/while/body/eval_jaxpr/tr,taw->raw/dot_general | solution.py:30
  422.8 6.6 copy.11
  429.5 131.3 %reduce-scatter.8.cloned.1.call-done = f32[256,128]{1,0:T(8,128)} async-done(((f32[4096,128]{1,0:T(8,128)}), f32[256,128]{1,0:T(8,128)}) %reduce-scatter.8.cloned.1.call-update) | async-done | bytes 131088 | tf_op jit(solution)/shard_map/reduce_scatter | solution.py:92
  565.2 67.1 %reduce-scatter.6.cloned.1.call-done = f32[256,256]{1,0:T(8,128)} async-done(((f32[4096,256]{1,0:T(8,128)}), f32[256,256]{1,0:T(8,128)}) %reduce-scatter.6.cloned.1.call-update) | async-done | bytes 262160 | tf_op jit(solution)/shard_map/reduce_scatter | solution.py:79
  634.2 254.5 %all-reduce.3.cloned.1.call-done = (f32[256,256]{1,0:T(8,128)}, f32[256,128]{1,0:T(8,128)}) async-done(((f32[256,256]{1,0:T(8,128)}, f32[256,128]{1,0:T(8,128)}), (f32[256,256]{1,0:T(8,128)}, f32[256,128]{1,0:T(8,128)})) %all-reduce.3.cloned.1.call-update) | async-done | bytes 393232 | tf_op jit(solution)/shard_map/psum | solution.py:100
  (113 shorter events, 83.8 us)
Async XLA Ops:
  7.2 226.8 %copy-start = (bf16[256,256]{1,0:T(8,128)(2,1)S(1)}, bf16[256,256]{1,0:T(8,128)(2,1)}, u32[]{:S(2)}) copy-start(bf16[256,256]{1,0:T(8,128)(2,1)} %param.19) | copy-start | bytes 393220
  7.2 89.2 %all-gather.4.cloned.1.call-start = ((), (), s32[]{:S(2)}) async-start(), calls=%async_computation.3 | async-start | bytes 2228224 | tf_op jit(solution)/shard_map/all_gather | solution.py:55
  7.9 226.1 %reduce-scatter.4.cloned.1.call-start = ((), (), s32[]{:S(2)}) async-start(), calls=%async_computation.4 | async-start | bytes 4456448 | tf_op jit(solution)/shard_map/reduce_scatter | solution.py:65
  167.7 105.5 %all-gather.8.cloned.1.call-start = ((), (), s32[]{:S(2)}) async-start(), calls=%async_computation.7 | async-start | bytes 1114112 | tf_op jit(solution)/shard_map/all_gather | solution.py:82
  168.4 189.4 %all-gather.6.cloned.1.call-start = ((), (), s32[]{:S(2)}) async-start(), calls=%async_computation.5 | async-start | bytes 2228224 | tf_op jit(solution)/shard_map/all_gather | solution.py:69
  235.9 324.9 %reduce-scatter.8.cloned.1.call-start = ((), (), s32[]{:S(2)}) async-start(), calls=%async_computation.8 | async-start | bytes 2228224 | tf_op jit(solution)/shard_map/reduce_scatter | solution.py:92
  313.0 319.3 %reduce-scatter.6.cloned.1.call-start = ((), (), s32[]{:S(2)}) async-start(), calls=%async_computation.6 | async-start | bytes 4456448 | tf_op jit(solution)/shard_map/reduce_scatter | solution.py:79
  429.4 131.4 %copy-start.1 = (bf16[256,256]{1,0:T(8,128)(2,1)S(1)}, bf16[256,256]{1,0:T(8,128)(2,1)}, u32[]{:S(2)}) copy-start(bf16[256,256]{1,0:T(8,128)(2,1)} %get-tuple-element.261) | copy-start | bytes 393220
  429.4 133.3 %copy-start.3 = (bf16[256,128]{1,0:T(8,128)(2,1)S(1)}, bf16[256,128]{1,0:T(8,128)(2,1)}, u32[]{:S(2)}) copy-start(bf16[256,128]{1,0:T(8,128)(2,1)} %param.20) | copy-start | bytes 196612
  429.4 134.5 %copy-start.2 = (f32[256,256]{1,0:T(8,128)S(1)}, f32[256,256]{1,0:T(8,128)}, u32[]{:S(2)}) copy-start(f32[256,256]{1,0:T(8,128)} %reduce-scatter.4.cloned.1.call-done) | copy-start | bytes 786436
  429.4 459.3 %all-reduce.3.cloned.1.call-start = ((), (), s32[]{:S(2)}) async-start(), calls=%async_computation.9 | async-start | bytes 786432 | tf_op jit(solution)/shard_map/psum | solution.py:100
Sparse Core Ops, SparseCore 0:
  10.6 85.6 all-gather.3
  167.8 66.1 reduce-scatter.3
  235.9 37.2 all-gather.7
  276.2 81.5 all-gather.5
  361.5 199.2 reduce-scatter.7
  563.2 69.0 reduce-scatter.5
  638.4 250.2 all-reduce.2
where the time goes:
time: 900 us; the launch traced here: 899 us
  waiting for transfers between devices  688 us (76%)
  matrix products  147 us (16%)
  local copies, waits for them, and re-layouts  47.9 us (5%)
  between operations  14.8 us (2%)
    psum x1, waiting for transfers between devices, on_device(): first_grad = lax.psum(first_local, ('row', 'col'))  255 us
    reduce_scatter x1, waiting for transfers between devices, on_device(): lax.psum_scatter(grad_part, 'col', scatter_dimension=0, tiled=True)  131 us
    dot_general x12, matrix products, add_group(): jnp.einsum('tr,taw->raw', select, products, precision=HIGHEST)  99.3 us
    all_gather x1, waiting for transfers between devices, on_device(): gathered_x = lax.all_gather(node_features, 'col', axis=0, tiled=True)  86.8 us
    reduce_scatter x1, waiting for transfers between devices, on_device(): lax.psum_scatter(hidden_part, 'row', scatter_dimension=0, tiled=True)  67.1 us
    reduce_scatter x1, waiting for transfers between devices, on_device(): lax.psum_scatter(feature_part, 'row', scatter_dimension=0, tiled=True)  65.5 us
    all_gather x1, waiting for transfers between devices, on_device(): gathered_h = lax.all_gather(hidden_act, 'col', axis=0, tiled=True)  44.8 us
    dot_general x12, matrix products, add_group(): jnp.einsum(einsum_form, group_tiles, picked, preferred_element_type=jnp.f...  39.1 us
  transfers between devices with their start and end apart: 7, of which 7 were waited for; matrix products, arithmetic and copies ran while one was open for 13% of the time, Pallas kernels for 0%

commit v1 on v0

--- a/solution.py
+++ b/solution.py
@@ -97,7 +97,7 @@
     pre_grad = hidden_grad * (sigma * (1.0 + first_pre * (1.0 - sigma)))
     second_grad = lax.psum(second_local, ("row", "col"))
     first_local = jnp.dot(first_mean.T, pre_grad, precision=HIGHEST) * scale
-    first_grad = lax.psum(first_local, ("row", "col"))
+    first_grad = lax.psum(lax.psum(first_local, "row"), "col")
     return (output, first_grad, second_grad)
 
 

time: 900 us -> 1140 us (1.27); the launches traced: 899 us -> 1130 us
  waiting for transfers between devices: 688 us -> 916 us
    psum x1 -> x3, waiting for transfers between devices: 255 us -> 446 us  [the longest x1 248 us: on_device(): second_grad = lax.psum(second_local, ('row', 'col'))]
    reduce_scatter x1, waiting for transfers between devices: 131 us -> 203 us  [on_device(): lax.psum_scatter(grad_part, 'col', scatter_dimension=0, tiled=True)]
    reduce_scatter x1, waiting for transfers between devices: 65.5 us -> 25.9 us  [on_device(): lax.psum_scatter(feature_part, 'row', scatter_dimension=0, tiled=True)]
    all_gather x1, waiting for transfers between devices: 44.8 us -> 84.3 us  [on_device(): gathered_h = lax.all_gather(hidden_act, 'col', axis=0, tiled=True)]
    all_gather x1, waiting for transfers between devices: 37 us -> 0.02 us  [on_device(): gathered_g = lax.all_gather(out_grad, 'row', axis=0, tiled=True)]
  transfers between devices with their start and end apart: 7 -> 9, of which waited for: 7 -> 8; matrix products, arithmetic and copies ran while one was open for 13% -> 17% of each run, Pallas kernels for 0% -> 0%
where the time goes in v1:
time: 1140 us; the launch traced here: 1130 us
  waiting for transfers between devices  916 us (80%)
  matrix products  146 us (13%)
  local copies, waits for them, and re-layouts  48.7 us (4%)
  between operations  14.6 us (1%)
    psum x1, waiting for transfers between devices, on_device(): second_grad = lax.psum(second_local, ('row', 'col'))  248 us
    reduce_scatter x1, waiting for transfers between devices, on_device(): lax.psum_scatter(grad_part, 'col', scatter_dimension=0, tiled=True)  203 us
    psum x2, waiting for transfers between devices, on_device(): first_grad = lax.psum(lax.psum(first_local, 'row'), 'col')  198 us
    dot_general x12, matrix products, add_group(): jnp.einsum('tr,taw->raw', select, products, precision=HIGHEST)  99.2 us
    all_gather x1, waiting for transfers between devices, on_device(): gathered_x = lax.all_gather(node_features, 'col', axis=0, tiled=True)  86 us
    all_gather x1, waiting for transfers between devices, on_device(): gathered_h = lax.all_gather(hidden_act, 'col', axis=0, tiled=True)  84.3 us
    reduce_scatter x1, waiting for transfers between devices, on_device(): lax.psum_scatter(hidden_part, 'row', scatter_dimension=0, tiled=True)  69.6 us
    dot_general x12, matrix products, add_group(): jnp.einsum(einsum_form, group_tiles, picked, preferred_element_type=jnp.f...  38.9 us
  transfers between devices with their start and end apart: 9, of which 8 were waited for; matrix products, arithmetic and copies ran while one was open for 17% of the time, Pallas kernels for 0%

profile of v1, /device:TPU:1, one launch (start us, length us, event | category | flops | bytes accessed | tf_op | source)
XLA Modules:
  0.0 1126.9 jit_solution(5448938369335001512)
XLA Ops:
  10.3 86.0 %all-gather.4.cloned.1.call-done = bf16[4096,256]{1,0:T(8,128)(2,1)} async-done(((bf16[256,256]{1,0:T(8,128)(2,1)}), bf16[4096,256]{1,0:T(8,128)(2,1)}) %all-gather.4.cloned.1.call-update) | async-done | bytes 2097168 | tf_op jit(solution)/shard_map/all_gather | solution.py:55
  96.3 64.6 %while.33 = (s32[]{:T(128)}, f32[32,128,256]{2,0,1:T(8,128)}, s32[4,32]{1,0:T(4,128)S(1)}, pred[4,32]{1,0:T(4,128)(4,1)S(1)}, bf16[4,32,128,128]{3,2,1,0:T(8,128...) while((s32[]{:T(128)}, f32[32,128,256]{2,0,1:T(8,128)}, ...), condition=%wide.region_1.3_spmd.clone, body=%wide.region_0.2_spmd.clone.sunk | while | flops 674237632 | bytes 24123028 | solution.py:34
  102.6 8.9 select_add_fusion.6
  117.8 10.2 select_add_fusion.6
  134.3 10.2 select_add_fusion.6
  150.8 10.2 select_add_fusion.6
  161.0 6.6 copy.10
  167.8 35.7 %while.35 = (s32[]{:T(128)}, f32[32,128,128]{2,0,1:T(8,128)}, s32[4,32]{1,0:T(4,128)S(1)}, pred[4,32]{1,0:T(4,128)(4,1)S(1)}, bf16[4,32,128,128]{3,2,1,0:T(8,128...) while((s32[]{:T(128)}, f32[32,128,128]{2,0,1:T(8,128)}, ...), condition=%wide.region_7.9_spmd.clone, body=%wide.region_6.8_spmd.clone.sunk | while | flops 337120544 | bytes 12588823 | solution.py:34
  179.4 5.5 select_add_fusion.8
  188.8 5.5 select_add_fusion.8
  198.1 5.4 select_add_fusion.8
  207.8 25.9 %reduce-scatter.4.cloned.1.call-done = f32[256,256]{1,0:T(8,128)} async-done(((f32[4096,256]{1,0:T(8,128)}), f32[256,256]{1,0:T(8,128)}) %reduce-scatter.4.cloned.1.call-update) | async-done | bytes 262160 | tf_op jit(solution)/shard_map/reduce_scatter | solution.py:65
  235.8 202.9 %reduce-scatter.8.cloned.1.call-done = f32[256,128]{1,0:T(8,128)} async-done(((f32[4096,128]{1,0:T(8,128)}), f32[256,128]{1,0:T(8,128)}) %reduce-scatter.8.cloned.1.call-update) | async-done | bytes 131088 | tf_op jit(solution)/shard_map/reduce_scatter | solution.py:92
  442.4 84.3 %all-gather.6.cloned.1.call-done = bf16[4096,256]{1,0:T(8,128)(2,1)} async-done(((bf16[256,256]{1,0:T(8,128)(2,1)}), bf16[4096,256]{1,0:T(8,128)(2,1)}) %all-gather.6.cloned.1.call-update) | async-done | bytes 2097168 | tf_op jit(solution)/shard_map/all_gather | solution.py:69
  526.7 64.7 %while.34 = (s32[]{:T(128)}, f32[32,128,256]{2,0,1:T(8,128)}, s32[4,32]{1,0:T(4,128)S(1)}, pred[4,32]{1,0:T(4,128)(4,1)S(1)}, bf16[4,32,128,128]{3,2,1,0:T(8,128...) while((s32[]{:T(128)}, f32[32,128,256]{2,0,1:T(8,128)}, ...), condition=%wide.region_4.6_spmd.clone, body=%wide.region_3.5_spmd.clone.sunk | while | flops 674237632 | bytes 24123028 | solution.py:34
  533.0 8.9 select_add_fusion.7
  548.2 10.2 select_add_fusion.7
  564.7 10.2 select_add_fusion.7
  581.2 10.2 select_add_fusion.7
  591.4 6.6 copy.11
  600.0 51.6 %all-reduce.4.cloned.1.call-done = f32[256,256]{1,0:T(8,128)} async-done(((f32[256,256]{1,0:T(8,128)}), f32[256,256]{1,0:T(8,128)}) %all-reduce.4.cloned.1.call-update) | async-done | bytes 262160 | tf_op jit(solution)/shard_map/psum | solution.py:100
  651.7 69.6 %reduce-scatter.6.cloned.1.call-done = f32[256,256]{1,0:T(8,128)} async-done(((f32[4096,256]{1,0:T(8,128)}), f32[256,256]{1,0:T(8,128)}) %reduce-scatter.6.cloned.1.call-update) | async-done | bytes 262160 | tf_op jit(solution)/shard_map/reduce_scatter | solution.py:79
  723.1 248.1 %all-reduce.8.cloned.1.call-done = f32[256,128]{1,0:T(8,128)} async-done(((f32[256,128]{1,0:T(8,128)}), f32[256,128]{1,0:T(8,128)}) %all-reduce.8.cloned.1.call-update) | async-done | bytes 131088 | tf_op jit(solution)/shard_map/psum | solution.py:98
  971.2 145.9 %all-reduce.6.cloned.1.call-done = f32[256,256]{1,0:T(8,128)} async-done(((f32[256,256]{1,0:T(8,128)}), f32[256,256]{1,0:T(8,128)}) %all-reduce.6.cloned.1.call-update) | async-done | bytes 262160 | tf_op jit(solution)/shard_map/psum | solution.py:100
  (119 shorter events, 89.0 us)
Async XLA Ops:
  7.2 226.6 %copy-start = (bf16[256,256]{1,0:T(8,128)(2,1)S(1)}, bf16[256,256]{1,0:T(8,128)(2,1)}, u32[]{:S(2)}) copy-start(bf16[256,256]{1,0:T(8,128)(2,1)} %param.19) | copy-start | bytes 393220
  7.2 89.2 %all-gather.4.cloned.1.call-start = ((), (), s32[]{:S(2)}) async-start(), calls=%async_computation.3 | async-start | bytes 2228224 | tf_op jit(solution)/shard_map/all_gather | solution.py:55
  7.9 159.9 %all-gather.8.cloned.1.call-start = ((), (), s32[]{:S(2)}) async-start(), calls=%async_computation.7 | async-start | bytes 1114112 | tf_op jit(solution)/shard_map/all_gather | solution.py:82
  8.7 225.1 %reduce-scatter.4.cloned.1.call-start = ((), (), s32[]{:S(2)}) async-start(), calls=%async_computation.4 | async-start | bytes 4456448 | tf_op jit(solution)/shard_map/reduce_scatter | solution.py:65
  167.6 271.1 %reduce-scatter.8.cloned.1.call-start = ((), (), s32[]{:S(2)}) async-start(), calls=%async_computation.8 | async-start | bytes 2228224 | tf_op jit(solution)/shard_map/reduce_scatter | solution.py:92
  203.6 235.1 %copy-start.3 = (bf16[256,128]{1,0:T(8,128)(2,1)S(1)}, bf16[256,128]{1,0:T(8,128)(2,1)}, u32[]{:S(2)}) copy-start(bf16[256,128]{1,0:T(8,128)(2,1)} %param.20) | copy-start | bytes 196612
  207.8 318.9 %all-gather.6.cloned.1.call-start = ((), (), s32[]{:S(2)}) async-start(), calls=%async_computation.5 | async-start | bytes 2228224 | tf_op jit(solution)/shard_map/all_gather | solution.py:69
  235.7 415.9 %all-reduce.4.cloned.1.call-start = ((), (), s32[]{:S(2)}) async-start(), calls=%async_computation.9 | async-start | bytes 524288 | tf_op jit(solution)/shard_map/psum | solution.py:100
  442.1 279.1 %reduce-scatter.6.cloned.1.call-start = ((), (), s32[]{:S(2)}) async-start(), calls=%async_computation.6 | async-start | bytes 4456448 | tf_op jit(solution)/shard_map/reduce_scatter | solution.py:79
  598.0 0.9 copy-start.1
  598.0 1.0 copy-start.2
  598.0 373.2 %all-reduce.8.cloned.1.call-start = ((), (), s32[]{:S(2)}) async-start(), calls=%async_computation.11 | async-start | bytes 262144 | tf_op jit(solution)/shard_map/psum | solution.py:98
  600.0 517.2 %all-reduce.6.cloned.1.call-start = ((), (), s32[]{:S(2)}) async-start(), calls=%async_computation.10 | async-start | bytes 524288 | tf_op jit(solution)/shard_map/psum | solution.py:100
Sparse Core Ops, SparseCore 0:
  10.6 85.6 all-gather.3
  98.2 35.5 all-gather.7
  167.7 66.0 reduce-scatter.3
  237.5 201.1 reduce-scatter.7
  441.7 85.0 all-gather.5
  529.8 121.8 all-reduce.3
  654.3 66.8 reduce-scatter.5
  728.2 242.8 all-reduce.7
  974.0 143.0 all-reduce.5
